TPU v7x, 256 devices: a whole 4x4x8 slice. The times are simulated.
256 devices in a mesh: row: 8 (over x, core), col: 32 (over y, z).
Axes of the slice: x: 4, y: 4, z: 8, core: 2. Of those that a mesh axis runs over, the one named last changes fastest.
Arguments:
- factor: float32 [6, 8, 32, 512, 512], P(None, 'row', 'col'), may hold values from -0.1875 to 0.1875
- rhs: float32 [6, 8, 32, 128, 128], P(None, 'row', 'col'), may hold values from -6 to 6
- inverses: float32 [4, 512, 512], replicated, may hold values from -0.5 to 2, as said below
Outputs:
- solved: float32 [4, 512, 128], P(None, 'col')
- remaining: float32 [6, 8, 32, 128, 128], P(None, 'row', 'col')
Inputs may be any that keep to these rules, and one draw needn't show every extreme that they name: `inverses`: each block is lower triangular with its diagonal between 0.5 and 2 and entries below it of magnitude at most 4 / sqrt(512).
All inputs are finite; a program needn't handle non-finite values.
Results may differ from a plain program's by a relative error of at most 0.00011.
Values sent between devices are 32-bit elements; how exact they have to be, the bound alone decides.
A program may use at most 64 MiB of HBM per device.

v0:
```python
import jax
import jax.numpy as jnp
from jax import lax
from jax.sharding import PartitionSpec as P


def shifted(block, axis, distance):
    devices = range(lax.axis_size(axis))
    route = [((i - distance) % len(devices), i) for i in devices]
    return lax.ppermute(block, axis, route)


def broadcast(x, axis, root):
    mine = lax.axis_index(axis) == root
    return lax.psum(jnp.where(mine, x, jnp.zeros_like(x)), axis)


def group_reduce(update, member, steps, groups):
    blocks = update.shape[0]
    nrhs = update.shape[2]
    split = update.reshape(blocks, steps, update.shape[1] // steps, nrhs)
    total = lax.dynamic_index_in_dim(split, member, 1, keepdims=False)
    for offset in range(1, steps):
        piece = lax.dynamic_index_in_dim(split, (member + offset) % steps, 1, keepdims=False)
        total = total + shifted(piece, "col", offset * groups)
    return total


def on_device(factor, rhs, inverses):
    steps = inverses.shape[0]
    blocks = factor.shape[0]
    width = factor.shape[3]
    quarter = rhs.shape[3]
    nrhs = rhs.shape[4]
    row_count = lax.axis_size("row")
    col_count = lax.axis_size("col")
    groups = col_count // steps
    row_pos = lax.axis_index("row")
    col_pos = lax.axis_index("col")
    member = col_pos // groups
    group = col_pos % groups
    block_ids = (jnp.arange(blocks, dtype=jnp.int32) * row_count + row_pos) * groups + group
    panel = factor[:, 0, 0]
    current = rhs[:, 0, 0]
    solved_list = []
    for k in range(steps):
        owner_row = k // groups
        owner_group = k % groups
        placed = lax.dynamic_update_slice(
            jnp.zeros((width, nrhs), jnp.float32),
            current[0],
            (member * quarter, jnp.zeros((), jnp.int32)),
        )
        contrib = placed
        is_owner = jnp.logical_and(row_pos == owner_row, group == owner_group)
        contrib = jnp.where(is_owner, contrib, jnp.zeros_like(contrib))
        complete = lax.psum(contrib, "col")
        solved_block = jnp.dot(inverses[k], complete, precision=lax.Precision.HIGHEST)
        solved_block = broadcast(solved_block, "row", owner_row)
        solved_list.append(solved_block)
        keep = (block_ids > k).astype(jnp.float32)[:, None, None]

        def column_update(solved_now=solved_block, keep_now=keep):
            return (
                jnp.einsum("rji,jh->rih", panel, solved_now, precision=lax.Precision.HIGHEST)
                * keep_now
            )

        def no_update():
            return jnp.zeros((blocks, width, nrhs), jnp.float32)

        update = lax.cond(member == k, column_update, no_update)
        current = current - group_reduce(update, member, steps, groups)
    stacked = jnp.stack(solved_list)
    share = width // col_count
    solved_rows = lax.dynamic_slice_in_dim(stacked, col_pos * share, share, 1)
    return (solved_rows, current[:, None, None])


def solution(mesh):
    in_specs = (P(None, "row", "col", None, None), P(None, "row", "col", None, None), P())
    out_specs = (P(None, "col", None), P(None, "row", "col", None, None))
    return jax.shard_map(
        on_device, mesh=mesh, in_specs=in_specs, out_specs=out_specs, check_vma=False
    )
```

profile of v0, /device:TPU:7, one launch (start us, length us, event | category | flops | bytes accessed | tf_op | source)
XLA Modules:
  0.0 980.9 jit_solution(4131290574086656395)
XLA Ops:
  7.2 0.0 all-reduce.9.cloned.1.call-start
  7.3 0.9 bitcast_dynamic-update-slice_fusion
  8.1 0.7 copy-done.5
  8.9 0.0 all-reduce.11.cloned.1.call-start
  9.0 6.6 copy.5
  15.6 139.2 %all-reduce.9.cloned.1.call-done = f32[512,128]{1,0:T(8,128)} async-done(((f32[512,128]{1,0:T(8,128)}), f32[512,128]{1,0:T(8,128)}) %all-reduce.9.cloned.1.call-update) | async-done | bytes 262160 | tf_op jit(solution)/shard_map/psum | solution.py:57
  154.7 3.3 fusion.7
  158.0 0.0 all-reduce.11.cloned.1.call-update
  158.0 0.0 all-reduce.13.cloned.1.call-start
  158.1 65.0 %all-reduce.11.cloned.1.call-done = f32[512,128]{0,1:T(8,128)} async-done(((f32[512,128]{0,1:T(8,128)}), f32[512,128]{0,1:T(8,128)}) %all-reduce.11.cloned.1.call-update) | async-done | bytes 262160 | tf_op jit(solution)/shard_map/psum | solution.py:15
  223.1 7.2 conditional.4
  223.1 7.2 convolution_multiply_fusion
  230.3 0.9 dynamic-slice_bitcast_fusion.11
  231.2 2.7 collective-permute-start.2
  233.8 18.1 %collective-permute-done = f32[6,128,128]{2,1,0:T(8,128)S(1)} collective-permute-done((f32[6,128,128]{2,1,0:T(8,128)}, f32[6,128,128]{2,1,0:T(8,128)S(1)}, u32[]{:S(2)}, u32[]{:S(2)}) %collective-permute-start) | collective-permute-done | bytes 393248 | tf_op jit(solution)/shard_map/ppermute | solution.py:10
  251.9 0.3 collective-permute-done.2
  252.2 1.1 fusion.28
  253.4 0.7 copy-done.6
  254.0 0.0 all-reduce.13.cloned.1.call-update
  254.1 0.0 all-reduce.15.cloned.1.call-start
  254.1 140.4 %all-reduce.13.cloned.1.call-done = f32[512,128]{1,0:T(8,128)} async-done(((f32[512,128]{1,0:T(8,128)}), f32[512,128]{1,0:T(8,128)}) %all-reduce.13.cloned.1.call-update) | async-done | bytes 262160 | tf_op jit(solution)/shard_map/psum | solution.py:57
  394.5 3.3 fusion.6
  397.8 0.0 all-reduce.17.cloned.1.call-start
  397.8 65.0 %all-reduce.15.cloned.1.call-done = f32[512,128]{0,1:T(8,128)} async-done(((f32[512,128]{0,1:T(8,128)}), f32[512,128]{0,1:T(8,128)}) %all-reduce.15.cloned.1.call-update) | async-done | bytes 262160 | tf_op jit(solution)/shard_map/psum | solution.py:15
  462.9 0.2 conditional.5
  462.9 0.2 reshape.83
  463.1 0.9 dynamic-slice_bitcast_fusion.8
  463.9 8.2 collective-permute-start.3
  472.1 2.4 collective-permute-start.5
  474.5 6.6 collective-permute-done.3
  481.1 8.3 collective-permute-done.4
  489.4 0.8 collective-permute-done.5
  490.3 1.1 fusion.25
  491.4 0.7 copy-done.7
  492.2 0.0 all-reduce.19.cloned.1.call-start
  492.2 141.5 %all-reduce.17.cloned.1.call-done = f32[512,128]{1,0:T(8,128)} async-done(((f32[512,128]{1,0:T(8,128)}), f32[512,128]{1,0:T(8,128)}) %all-reduce.17.cloned.1.call-update) | async-done | bytes 262160 | tf_op jit(solution)/shard_map/psum | solution.py:57
  633.7 3.3 fusion.5
  637.0 0.0 all-reduce.21.cloned.1.call-start
  637.0 65.1 %all-reduce.19.cloned.1.call-done = f32[512,128]{0,1:T(8,128)} async-done(((f32[512,128]{0,1:T(8,128)}), f32[512,128]{0,1:T(8,128)}) %all-reduce.19.cloned.1.call-update) | async-done | bytes 262160 | tf_op jit(solution)/shard_map/psum | solution.py:15
  702.1 0.2 conditional.6
  702.1 0.2 reshape.85
  702.3 0.9 dynamic-slice_bitcast_fusion.5
  703.1 1.2 collective-permute-start.6
  704.3 8.5 collective-permute-start.7
  712.9 2.1 collective-permute-start.8
  714.9 0.5 collective-permute-done.6
  715.4 15.7 %collective-permute-done.7 = f32[6,128,128]{2,1,0:T(8,128)S(1)} collective-permute-done((f32[6,128,128]{2,1,0:T(8,128)S(1)}, f32[6,128,128]{2,1,0:T(8,128)S(1)}, u32[]{:S(2)}, u32[]{:S(2)}) %collective-permute-start.7) | collective-permute-done | bytes 393248 | tf_op jit(solution)/shard_map/ppermute | solution.py:10
  731.1 1.1 fusion.22
  732.3 0.7 copy-done.4
  733.0 0.0 all-reduce.23.cloned.1.call-start
  733.0 141.1 %all-reduce.21.cloned.1.call-done = f32[512,128]{1,0:T(8,128)} async-done(((f32[512,128]{1,0:T(8,128)}), f32[512,128]{1,0:T(8,128)}) %all-reduce.21.cloned.1.call-update) | async-done | bytes 262160 | tf_op jit(solution)/shard_map/psum | solution.py:57
  874.1 3.3 fusion.4
  877.4 65.1 %all-reduce.23.cloned.1.call-done = f32[512,128]{0,1:T(8,128)} async-done(((f32[512,128]{0,1:T(8,128)}), f32[512,128]{0,1:T(8,128)}) %all-reduce.23.cloned.1.call-update) | async-done | bytes 262160 | tf_op jit(solution)/shard_map/psum | solution.py:15
  942.5 0.2 conditional.7
  942.5 0.2 reshape.87
  942.7 1.1 dynamic-slice_bitcast_fusion.2
  943.8 2.7 collective-permute-start.10
  946.5 6.7 collective-permute-start.11
  953.2 0.6 collective-permute-start.9
  953.8 0.1 fusion.31
  954.0 0.7 copy.10
  954.7 1.8 collective-permute-done.10
  956.5 15.5 %collective-permute-done.11 = f32[6,128,128]{2,1,0:T(8,128)} collective-permute-done((f32[6,128,128]{2,1,0:T(8,128)}, f32[6,128,128]{2,1,0:T(8,128)}, u32[]{:S(2)}, u32[]{:S(2)}) %collective-permute-start.11) | collective-permute-done | bytes 393248 | tf_op jit(solution)/shard_map/ppermute | solution.py:10
  972.0 2.1 fusion.19
  (35 shorter events, 0.3 us)
Async XLA Ops:
  7.2 147.6 %all-reduce.9.cloned.1.call-start = ((), (), s32[]{:S(2)}) async-start(), calls=%async_computation | async-start | bytes 524288 | tf_op jit(solution)/shard_map/psum | solution.py:57
  8.1 0.7 copy-start.5
  8.9 214.3 %all-reduce.11.cloned.1.call-start = ((), (), s32[]{:S(2)}) async-start(), calls=%async_computation.1 | async-start | bytes 524288 | tf_op jit(solution)/shard_map/psum | solution.py:15
  158.0 236.5 %all-reduce.13.cloned.1.call-start = ((), (), s32[]{:S(2)}) async-start(), calls=%async_computation.2 | async-start | bytes 524288 | tf_op jit(solution)/shard_map/psum | solution.py:57
  230.3 21.9 %copy-start.8 = (f32[6,1,1,128,128]{4,3,2,1,0:T(8,128)S(1)}, f32[6,1,1,128,128]{4,3,2,1,0:T(8,128)}, u32[]{:S(2)}) copy-start(f32[6,1,1,128,128]{4,3,2,1,0:T(8,128)} %param.12) | copy-start | bytes 1179652
  231.1 20.7 %collective-permute-start = (f32[6,128,128]{2,1,0:T(8,128)}, f32[6,128,128]{2,1,0:T(8,128)S(1)}, u32[]{:S(2)}, u32[]{:S(2)}) collective-permute-start(f32[6,128,128]{2,1,0:T(8,128)} %get-tuple-element.79), channel_id=1, source_target_pairs={{24,0},{25,1},{26,2},{27,3},{28,4},{29,5},{30,6},{31,7},{0,8},{1,9... | collective-permute-start | bytes 1179656 | tf_op jit(solution)/shard_map/ppermute | solution.py:10
  231.1 20.7 %collective-permute-start.1 = (f32[6,128,128]{2,1,0:T(8,128)S(1)}, f32[6,128,128]{2,1,0:T(8,128)S(1)}, u32[]{:S(2)}, u32[]{:S(2)}) collective-permute-start(f32[6,128,128]{2,1,0:T(8,128)S(1)} %get-tuple-element.81), channel_id=1, source_target_pairs={{16,0},{17,1},{18,2},{19,3},{20,4},{21,5},{22,6},{23,7},{24,8},{25... | collective-permute-start | bytes 1179656 | tf_op jit(solution)/shard_map/ppermute | solution.py:10
  231.2 21.0 %collective-permute-start.2 = (f32[6,128,128]{2,1,0:T(8,128)S(1)}, f32[6,128,128]{2,1,0:T(8,128)}, u32[]{:S(2)}, u32[]{:S(2)}) collective-permute-start(f32[6,128,128]{2,1,0:T(8,128)S(1)} %get-tuple-element.80), channel_id=1, source_target_pairs={{8,0},{9,1},{10,2},{11,3},{12,4},{13,5},{14,6},{15,7},{16,8},{17,9... | collective-permute-start | bytes 1179656 | tf_op jit(solution)/shard_map/ppermute | solution.py:10
  253.3 0.7 copy-start.6
  254.1 208.8 %all-reduce.15.cloned.1.call-start = ((), (), s32[]{:S(2)}) async-start(), calls=%async_computation.3 | async-start | bytes 524288 | tf_op jit(solution)/shard_map/psum | solution.py:15
  397.8 235.9 %all-reduce.17.cloned.1.call-start = ((), (), s32[]{:S(2)}) async-start(), calls=%async_computation.4 | async-start | bytes 524288 | tf_op jit(solution)/shard_map/psum | solution.py:57
  463.9 17.2 %collective-permute-start.3 = (f32[6,128,128]{2,1,0:T(8,128)}, f32[6,128,128]{2,1,0:T(8,128)S(1)}, u32[]{:S(2)}, u32[]{:S(2)}) collective-permute-start(f32[6,128,128]{2,1,0:T(8,128)} %get-tuple-element.76), channel_id=1, source_target_pairs={{24,0},{25,1},{26,2},{27,3},{28,4},{29,5},{30,6},{31,7},{0,8},{1,9... | collective-permute-start | bytes 1179656 | tf_op jit(solution)/shard_map/ppermute | solution.py:10
  472.1 17.3 %collective-permute-start.4 = (f32[6,128,128]{2,1,0:T(8,128)S(1)}, f32[6,128,128]{2,1,0:T(8,128)S(1)}, u32[]{:S(2)}, u32[]{:S(2)}) collective-permute-start(f32[6,128,128]{2,1,0:T(8,128)S(1)} %get-tuple-element.78), channel_id=1, source_target_pairs={{16,0},{17,1},{18,2},{19,3},{20,4},{21,5},{22,6},{23,7},{24,8},{25... | collective-permute-start | bytes 1179656 | tf_op jit(solution)/shard_map/ppermute | solution.py:10
  472.1 18.2 %collective-permute-start.5 = (f32[6,128,128]{2,1,0:T(8,128)S(1)}, f32[6,128,128]{2,1,0:T(8,128)}, u32[]{:S(2)}, u32[]{:S(2)}) collective-permute-start(f32[6,128,128]{2,1,0:T(8,128)S(1)} %get-tuple-element.77), channel_id=1, source_target_pairs={{8,0},{9,1},{10,2},{11,3},{12,4},{13,5},{14,6},{15,7},{16,8},{17,9... | collective-permute-start | bytes 1179656 | tf_op jit(solution)/shard_map/ppermute | solution.py:10
  491.4 0.7 copy-start.7
  492.2 209.9 %all-reduce.19.cloned.1.call-start = ((), (), s32[]{:S(2)}) async-start(), calls=%async_computation.5 | async-start | bytes 524288 | tf_op jit(solution)/shard_map/psum | solution.py:15
  637.0 237.1 %all-reduce.21.cloned.1.call-start = ((), (), s32[]{:S(2)}) async-start(), calls=%async_computation.6 | async-start | bytes 524288 | tf_op jit(solution)/shard_map/psum | solution.py:57
  703.1 12.3 %collective-permute-start.6 = (f32[6,128,128]{2,1,0:T(8,128)}, f32[6,128,128]{2,1,0:T(8,128)S(1)}, u32[]{:S(2)}, u32[]{:S(2)}) collective-permute-start(f32[6,128,128]{2,1,0:T(8,128)} %get-tuple-element.73), channel_id=1, source_target_pairs={{24,0},{25,1},{26,2},{27,3},{28,4},{29,5},{30,6},{31,7},{0,8},{1,9... | collective-permute-start | bytes 1179656 | tf_op jit(solution)/shard_map/ppermute | solution.py:10
  704.3 26.8 %collective-permute-start.7 = (f32[6,128,128]{2,1,0:T(8,128)S(1)}, f32[6,128,128]{2,1,0:T(8,128)S(1)}, u32[]{:S(2)}, u32[]{:S(2)}) collective-permute-start(f32[6,128,128]{2,1,0:T(8,128)S(1)} %get-tuple-element.75), channel_id=1, source_target_pairs={{16,0},{17,1},{18,2},{19,3},{20,4},{21,5},{22,6},{23,7},{24,8},{25... | collective-permute-start | bytes 1179656 | tf_op jit(solution)/shard_map/ppermute | solution.py:10
  712.9 18.2 %collective-permute-start.8 = (f32[6,128,128]{2,1,0:T(8,128)S(1)}, f32[6,128,128]{2,1,0:T(8,128)}, u32[]{:S(2)}, u32[]{:S(2)}) collective-permute-start(f32[6,128,128]{2,1,0:T(8,128)S(1)} %get-tuple-element.74), channel_id=1, source_target_pairs={{8,0},{9,1},{10,2},{11,3},{12,4},{13,5},{14,6},{15,7},{16,8},{17,9... | collective-permute-start | bytes 1179656 | tf_op jit(solution)/shard_map/ppermute | solution.py:10
  732.2 0.7 copy-start.4
  733.0 209.5 %all-reduce.23.cloned.1.call-start = ((), (), s32[]{:S(2)}) async-start(), calls=%async_computation.7 | async-start | bytes 524288 | tf_op jit(solution)/shard_map/psum | solution.py:15
  942.7 11.1 %copy-start = (f32[512,128]{0,1:T(8,128)S(1)}, f32[512,128]{0,1:T(8,128)}, u32[]{:S(2)}) copy-start(f32[512,128]{0,1:T(8,128)} %all-reduce.11.cloned.1.call-done) | copy-start | bytes 786436
  942.7 11.1 %copy-start.1 = (f32[512,128]{0,1:T(8,128)S(1)}, f32[512,128]{0,1:T(8,128)}, u32[]{:S(2)}) copy-start(f32[512,128]{0,1:T(8,128)} %all-reduce.15.cloned.1.call-done) | copy-start | bytes 786436
  942.7 11.1 %copy-start.2 = (f32[512,128]{0,1:T(8,128)S(1)}, f32[512,128]{0,1:T(8,128)}, u32[]{:S(2)}) copy-start(f32[512,128]{0,1:T(8,128)} %all-reduce.19.cloned.1.call-done) | copy-start | bytes 786436
  942.7 11.1 %copy-start.3 = (f32[512,128]{0,1:T(8,128)S(1)}, f32[512,128]{0,1:T(8,128)}, u32[]{:S(2)}) copy-start(f32[512,128]{0,1:T(8,128)} %all-reduce.23.cloned.1.call-done) | copy-start | bytes 786436
  943.8 12.7 %collective-permute-start.10 = (f32[6,128,128]{2,1,0:T(8,128)}, f32[6,128,128]{2,1,0:T(8,128)}, u32[]{:S(2)}, u32[]{:S(2)}) collective-permute-start(f32[6,128,128]{2,1,0:T(8,128)} %get-tuple-element.72), channel_id=1, source_target_pairs={{16,0},{17,1},{18,2},{19,3},{20,4},{21,5},{22,6},{23,7},{24,8},{25... | collective-permute-start | bytes 1179656 | tf_op jit(solution)/shard_map/ppermute | solution.py:10
  946.5 25.5 %collective-permute-start.11 = (f32[6,128,128]{2,1,0:T(8,128)}, f32[6,128,128]{2,1,0:T(8,128)}, u32[]{:S(2)}, u32[]{:S(2)}) collective-permute-start(f32[6,128,128]{2,1,0:T(8,128)} %get-tuple-element.71), channel_id=1, source_target_pairs={{8,0},{9,1},{10,2},{11,3},{12,4},{13,5},{14,6},{15,7},{16,8},{17,9... | collective-permute-start | bytes 1179656 | tf_op jit(solution)/shard_map/ppermute | solution.py:10
  953.2 18.8 %collective-permute-start.9 = (f32[6,128,128]{2,1,0:T(8,128)}, f32[6,128,128]{2,1,0:T(8,128)}, u32[]{:S(2)}, u32[]{:S(2)}) collective-permute-start(f32[6,128,128]{2,1,0:T(8,128)} %get-tuple-element.70), channel_id=1, source_target_pairs={{24,0},{25,1},{26,2},{27,3},{28,4},{29,5},{30,6},{31,7},{0,8},{1,9... | collective-permute-start | bytes 1179656 | tf_op jit(solution)/shard_map/ppermute | solution.py:10
Sparse Core Ops, SparseCore 0:
  12.0 142.6 all-reduce.8
  158.1 64.9 all-reduce.10
  254.2 140.2 all-reduce.12
  397.9 64.9 all-reduce.14
  492.3 141.3 all-reduce.16
  637.1 64.9 all-reduce.18
  733.1 140.9 all-reduce.20
  877.5 64.9 all-reduce.22
where the time goes:
time: 981 us
  waiting for transfers between devices  890 us (91%)
  starting transfers between devices  35.4 us (4%)
  matrix products  20.2 us (2%)
  between operations  14.4 us (1%)
  local copies, waits for them, and re-layouts  14.3 us (1%)
    psum x4, waiting for transfers between devices, on_device(): complete = lax.psum(contrib, 'col')  562 us
    psum x4, waiting for transfers between devices, broadcast(): return lax.psum(jnp.where(mine, x, jnp.zeros_like(x)), axis)  260 us
    ppermute x12, waiting for transfers between devices, shifted(): return lax.ppermute(block, axis, route)  67.6 us
    ppermute x12, starting transfers between devices, shifted(): return lax.ppermute(block, axis, route)  35.1 us
  transfers between devices with their start and end apart: 20, of which 17 were waited for; matrix products, arithmetic and copies ran while one was open for 1% of the time, Pallas kernels for 0%

commit v1 on v0

--- a/solution.py
+++ b/solution.py
@@ -2,6 +2,12 @@
 import jax.numpy as jnp
 from jax import lax
 from jax.sharding import PartitionSpec as P
+
+
+def add_all(x, axis):
+    terms = lax.all_gather(x, axis, axis=0, tiled=False)
+    acc = terms.sum(axis=0)
+    return acc
 
 
 def shifted(block, axis, distance):
@@ -12,7 +18,7 @@
 
 def broadcast(x, axis, root):
     mine = lax.axis_index(axis) == root
-    return lax.psum(jnp.where(mine, x, jnp.zeros_like(x)), axis)
+    return add_all(jnp.where(mine, x, jnp.zeros_like(x)), axis)
 
 
 def group_reduce(update, member, steps, groups):

time: 981 us -> 855 us (0.87)
  waiting for transfers between devices: 890 us -> 745 us
  local copies, waits for them, and re-layouts: 14.3 us -> 27.6 us
    psum x4 -> x0, waiting for transfers between devices: 260 us -> none  [broadcast(): return lax.psum(jnp.where(mine, x, jnp.zeros_like(x)), axis)]
    all_gather x0 -> x4, waiting for transfers between devices: none -> 108 us  [add_all(): terms = lax.all_gather(x, axis, axis=0, tiled=False)]
    unnamed x20 -> x18, local copies, waits for them, and re-layouts: 10.1 us -> 23 us
  transfers between devices with their start and end apart: 20 -> 20, of which waited for: 17 -> 16; matrix products, arithmetic and copies ran while one was open for 1% -> 1% of each run, Pallas kernels for 0% -> 0%
where the time goes in v1:
time: 855 us; the launch traced here: 852 us
  waiting for transfers between devices  745 us (87%)
  starting transfers between devices  35.6 us (4%)
  local copies, waits for them, and re-layouts  27.6 us (3%)
  matrix products  20.2 us (2%)
  between operations  14.4 us (2%)
  other arithmetic  9.02 us (1%)
    psum x4, waiting for transfers between devices, on_device(): complete = lax.psum(contrib, 'col')  571 us
    all_gather x4, waiting for transfers between devices, add_all(): terms = lax.all_gather(x, axis, axis=0, tiled=False)  108 us
    ppermute x12, waiting for transfers between devices, shifted(): return lax.ppermute(block, axis, route)  66.6 us
    ppermute x12, starting transfers between devices, shifted(): return lax.ppermute(block, axis, route)  35.1 us
    unnamed x18, local copies, waits for them, and re-layouts  23 us
  transfers between devices with their start and end apart: 20, of which 16 were waited for; matrix products, arithmetic and copies ran while one was open for 1% of the time, Pallas kernels for 0%

profile of v1, /device:TPU:7, one launch (start us, length us, event | category | flops | bytes accessed | tf_op | source)
XLA Modules:
  0.0 852.5 jit_solution(14651620832224271785)
XLA Ops:
  7.3 0.9 bitcast_dynamic-update-slice_fusion
  8.1 0.7 copy-done.1
  8.9 0.0 all-gather.9.cloned.1.call-start
  8.9 145.8 %all-reduce.5.cloned.1.call-done = f32[512,128]{1,0:T(8,128)} async-done(((f32[512,128]{1,0:T(8,128)}), f32[512,128]{1,0:T(8,128)}) %all-reduce.5.cloned.1.call-update) | async-done | bytes 262160 | tf_op jit(solution)/shard_map/psum | solution.py:63
  154.7 3.3 fusion.7
  158.1 6.6 copy.6
  164.7 22.0 %all-gather.9.cloned.1.call-done = f32[4096,128]{0,1:T(8,128)} async-done(((f32[512,128]{0,1:T(8,128)}), f32[4096,128]{0,1:T(8,128)}) %all-gather.9.cloned.1.call-update) | async-done | bytes 2097168 | tf_op jit(solution)/shard_map/all_gather | solution.py:8
  186.7 3.2 copy.20
  189.9 0.5 bitcast_reduce_fusion.3
  190.5 7.2 conditional.4
  190.5 7.2 convolution_multiply_fusion
  197.7 1.0 dynamic-slice_bitcast_fusion.11
  198.7 2.7 collective-permute-start.2
  201.4 17.6 %collective-permute-done = f32[6,128,128]{2,1,0:T(8,128)S(1)} collective-permute-done((f32[6,128,128]{2,1,0:T(8,128)}, f32[6,128,128]{2,1,0:T(8,128)S(1)}, u32[]{:S(2)}, u32[]{:S(2)}) %collective-permute-start) | collective-permute-done | bytes 393248 | tf_op jit(solution)/shard_map/ppermute | solution.py:16
  219.0 0.5 collective-permute-done.2
  219.4 1.2 fusion.28
  220.7 0.7 copy-done.2
  221.5 140.9 %all-reduce.7.cloned.1.call-done = f32[512,128]{1,0:T(8,128)} async-done(((f32[512,128]{1,0:T(8,128)}), f32[512,128]{1,0:T(8,128)}) %all-reduce.7.cloned.1.call-update) | async-done | bytes 262160 | tf_op jit(solution)/shard_map/psum | solution.py:63
  362.4 3.3 fusion.6
  365.7 0.2 all-reduce.9.cloned.1.call-start
  365.9 28.5 %all-gather.11.cloned.1.call-done = f32[4096,128]{0,1:T(8,128)} async-done(((f32[512,128]{0,1:T(8,128)}), f32[4096,128]{0,1:T(8,128)}) %all-gather.11.cloned.1.call-update) | async-done | bytes 2097168 | tf_op jit(solution)/shard_map/all_gather | solution.py:8
  394.4 3.2 copy.21
  397.6 0.5 bitcast_reduce_fusion.2
  398.2 0.2 conditional.5
  398.2 0.2 reshape.83
  398.4 1.0 dynamic-slice_bitcast_fusion.8
  399.4 8.2 collective-permute-start.3
  407.6 2.4 collective-permute-start.5
  410.0 6.2 collective-permute-done.3
  416.1 8.4 collective-permute-done.4
  424.5 1.1 collective-permute-done.5
  425.6 1.2 fusion.25
  426.9 0.7 copy-done.3
  427.7 142.1 %all-reduce.9.cloned.1.call-done = f32[512,128]{1,0:T(8,128)} async-done(((f32[512,128]{1,0:T(8,128)}), f32[512,128]{1,0:T(8,128)}) %all-reduce.9.cloned.1.call-update) | async-done | bytes 262160 | tf_op jit(solution)/shard_map/psum | solution.py:63
  569.7 3.3 fusion.5
  573.1 28.7 %all-gather.13.cloned.1.call-done = f32[4096,128]{0,1:T(8,128)} async-done(((f32[512,128]{0,1:T(8,128)}), f32[4096,128]{0,1:T(8,128)}) %all-gather.13.cloned.1.call-update) | async-done | bytes 2097168 | tf_op jit(solution)/shard_map/all_gather | solution.py:8
  601.7 3.2 copy.22
  605.0 0.5 bitcast_reduce_fusion.1
  605.5 0.4 conditional.6
  605.5 0.2 reshape.85
  605.9 1.0 dynamic-slice_bitcast_fusion.5
  607.0 1.2 collective-permute-start.6
  608.2 8.5 %collective-permute-start.7 = (f32[6,128,128]{2,1,0:T(8,128)}, f32[6,128,128]{2,1,0:T(8,128)}, u32[]{:S(2)}, u32[]{:S(2)}) collective-permute-start(f32[6,128,128]{2,1,0:T(8,128)} %get-tuple-element.75), channel_id=1, source_target_pairs={{16,0},{17,1},{18,2},{19,3},{20,4},{21,5},{22,6},{23,7},{24,8},{25... | collective-permute-start | bytes 1179656 | tf_op jit(solution)/shard_map/ppermute | solution.py:16
  616.7 2.1 collective-permute-start.8
  618.8 0.0 collective-permute-done.6
  618.8 15.9 %collective-permute-done.7 = f32[6,128,128]{2,1,0:T(8,128)} collective-permute-done((f32[6,128,128]{2,1,0:T(8,128)}, f32[6,128,128]{2,1,0:T(8,128)}, u32[]{:S(2)}, u32[]{:S(2)}) %collective-permute-start.7) | collective-permute-done | bytes 393248 | tf_op jit(solution)/shard_map/ppermute | solution.py:16
  634.7 1.3 fusion.22
  636.1 0.7 copy-done
  636.9 141.8 %all-reduce.11.cloned.1.call-done = f32[512,128]{1,0:T(8,128)} async-done(((f32[512,128]{1,0:T(8,128)}), f32[512,128]{1,0:T(8,128)}) %all-reduce.11.cloned.1.call-update) | async-done | bytes 262160 | tf_op jit(solution)/shard_map/psum | solution.py:63
  778.7 3.3 fusion.4
  782.0 28.7 %all-gather.15.cloned.1.call-done = f32[4096,128]{0,1:T(8,128)} async-done(((f32[512,128]{0,1:T(8,128)}), f32[4096,128]{0,1:T(8,128)}) %all-gather.15.cloned.1.call-update) | async-done | bytes 2097168 | tf_op jit(solution)/shard_map/all_gather | solution.py:8
  810.7 3.2 copy.23
  814.0 0.5 bitcast_reduce_fusion
  814.5 0.2 conditional.7
  814.5 0.2 reshape.87
  814.7 1.1 dynamic-slice_bitcast_fusion.2
  815.8 2.7 collective-permute-start.10
  818.5 6.7 collective-permute-start.11
  825.2 0.6 collective-permute-start.9
  825.8 0.1 fusion.31
  825.9 0.7 copy.11
  826.7 1.3 collective-permute-done.10
  828.0 15.6 %collective-permute-done.11 = f32[6,128,128]{2,1,0:T(8,128)} collective-permute-done((f32[6,128,128]{2,1,0:T(8,128)}, f32[6,128,128]{2,1,0:T(8,128)}, u32[]{:S(2)}, u32[]{:S(2)}) %collective-permute-start.11) | collective-permute-done | bytes 393248 | tf_op jit(solution)/shard_map/ppermute | solution.py:16
  843.6 2.1 fusion.19
  (37 shorter events, 0.5 us)
Async XLA Ops:
  7.2 147.6 %all-reduce.5.cloned.1.call-start = ((), (), s32[]{:S(2)}) async-start(), calls=%async_computation | async-start | bytes 524288 | tf_op jit(solution)/shard_map/psum | solution.py:63
  8.1 0.7 copy-start.1
  8.9 177.9 %all-gather.9.cloned.1.call-start = ((), (), s32[]{:S(2)}) async-start(), calls=%async_computation.4 | async-start | bytes 2359296 | tf_op jit(solution)/shard_map/all_gather | solution.py:8
  158.0 204.4 %all-reduce.7.cloned.1.call-start = ((), (), s32[]{:S(2)}) async-start(), calls=%async_computation.1 | async-start | bytes 524288 | tf_op jit(solution)/shard_map/psum | solution.py:63
  197.7 21.8 %copy-start.4 = (f32[6,1,1,128,128]{4,3,2,1,0:T(8,128)S(1)}, f32[6,1,1,128,128]{4,3,2,1,0:T(8,128)}, u32[]{:S(2)}) copy-start(f32[6,1,1,128,128]{4,3,2,1,0:T(8,128)} %param.12) | copy-start | bytes 1179652
  198.7 20.3 %collective-permute-start = (f32[6,128,128]{2,1,0:T(8,128)}, f32[6,128,128]{2,1,0:T(8,128)S(1)}, u32[]{:S(2)}, u32[]{:S(2)}) collective-permute-start(f32[6,128,128]{2,1,0:T(8,128)} %get-tuple-element.79), channel_id=1, source_target_pairs={{24,0},{25,1},{26,2},{27,3},{28,4},{29,5},{30,6},{31,7},{0,8},{1,9... | collective-permute-start | bytes 1179656 | tf_op jit(solution)/shard_map/ppermute | solution.py:16
  198.7 20.3 %collective-permute-start.1 = (f32[6,128,128]{2,1,0:T(8,128)}, f32[6,128,128]{2,1,0:T(8,128)}, u32[]{:S(2)}, u32[]{:S(2)}) collective-permute-start(f32[6,128,128]{2,1,0:T(8,128)} %get-tuple-element.81), channel_id=1, source_target_pairs={{16,0},{17,1},{18,2},{19,3},{20,4},{21,5},{22,6},{23,7},{24,8},{25... | collective-permute-start | bytes 1179656 | tf_op jit(solution)/shard_map/ppermute | solution.py:16
  198.7 20.7 %collective-permute-start.2 = (f32[6,128,128]{2,1,0:T(8,128)S(1)}, f32[6,128,128]{2,1,0:T(8,128)}, u32[]{:S(2)}, u32[]{:S(2)}) collective-permute-start(f32[6,128,128]{2,1,0:T(8,128)S(1)} %get-tuple-element.80), channel_id=1, source_target_pairs={{8,0},{9,1},{10,2},{11,3},{12,4},{13,5},{14,6},{15,7},{16,8},{17,9... | collective-permute-start | bytes 1179656 | tf_op jit(solution)/shard_map/ppermute | solution.py:16
  220.7 0.7 copy-start.2
  221.4 173.0 %all-gather.11.cloned.1.call-start = ((), (), s32[]{:S(2)}) async-start(), calls=%async_computation.5 | async-start | bytes 2359296 | tf_op jit(solution)/shard_map/all_gather | solution.py:8
  365.7 204.1 %all-reduce.9.cloned.1.call-start = ((), (), s32[]{:S(2)}) async-start(), calls=%async_computation.2 | async-start | bytes 524288 | tf_op jit(solution)/shard_map/psum | solution.py:63
  399.4 16.8 %collective-permute-start.3 = (f32[6,128,128]{2,1,0:T(8,128)}, f32[6,128,128]{2,1,0:T(8,128)S(1)}, u32[]{:S(2)}, u32[]{:S(2)}) collective-permute-start(f32[6,128,128]{2,1,0:T(8,128)} %get-tuple-element.76), channel_id=1, source_target_pairs={{24,0},{25,1},{26,2},{27,3},{28,4},{29,5},{30,6},{31,7},{0,8},{1,9... | collective-permute-start | bytes 1179656 | tf_op jit(solution)/shard_map/ppermute | solution.py:16
  407.6 17.0 %collective-permute-start.4 = (f32[6,128,128]{2,1,0:T(8,128)}, f32[6,128,128]{2,1,0:T(8,128)}, u32[]{:S(2)}, u32[]{:S(2)}) collective-permute-start(f32[6,128,128]{2,1,0:T(8,128)} %get-tuple-element.78), channel_id=1, source_target_pairs={{16,0},{17,1},{18,2},{19,3},{20,4},{21,5},{22,6},{23,7},{24,8},{25... | collective-permute-start | bytes 1179656 | tf_op jit(solution)/shard_map/ppermute | solution.py:16
  407.6 18.1 %collective-permute-start.5 = (f32[6,128,128]{2,1,0:T(8,128)S(1)}, f32[6,128,128]{2,1,0:T(8,128)}, u32[]{:S(2)}, u32[]{:S(2)}) collective-permute-start(f32[6,128,128]{2,1,0:T(8,128)S(1)} %get-tuple-element.77), channel_id=1, source_target_pairs={{8,0},{9,1},{10,2},{11,3},{12,4},{13,5},{14,6},{15,7},{16,8},{17,9... | collective-permute-start | bytes 1179656 | tf_op jit(solution)/shard_map/ppermute | solution.py:16
  426.9 0.7 copy-start.3
  427.6 174.1 %all-gather.13.cloned.1.call-start = ((), (), s32[]{:S(2)}) async-start(), calls=%async_computation.6 | async-start | bytes 2359296 | tf_op jit(solution)/shard_map/all_gather | solution.py:8
  573.0 205.7 %all-reduce.11.cloned.1.call-start = ((), (), s32[]{:S(2)}) async-start(), calls=%async_computation.3 | async-start | bytes 524288 | tf_op jit(solution)/shard_map/psum | solution.py:63
  607.0 11.9 %collective-permute-start.6 = (f32[6,128,128]{2,1,0:T(8,128)}, f32[6,128,128]{2,1,0:T(8,128)S(1)}, u32[]{:S(2)}, u32[]{:S(2)}) collective-permute-start(f32[6,128,128]{2,1,0:T(8,128)} %get-tuple-element.73), channel_id=1, source_target_pairs={{24,0},{25,1},{26,2},{27,3},{28,4},{29,5},{30,6},{31,7},{0,8},{1,9... | collective-permute-start | bytes 1179656 | tf_op jit(solution)/shard_map/ppermute | solution.py:16
  608.2 26.6 %collective-permute-start.7 = (f32[6,128,128]{2,1,0:T(8,128)}, f32[6,128,128]{2,1,0:T(8,128)}, u32[]{:S(2)}, u32[]{:S(2)}) collective-permute-start(f32[6,128,128]{2,1,0:T(8,128)} %get-tuple-element.75), channel_id=1, source_target_pairs={{16,0},{17,1},{18,2},{19,3},{20,4},{21,5},{22,6},{23,7},{24,8},{25... | collective-permute-start | bytes 1179656 | tf_op jit(solution)/shard_map/ppermute | solution.py:16
  616.7 18.0 %collective-permute-start.8 = (f32[6,128,128]{2,1,0:T(8,128)}, f32[6,128,128]{2,1,0:T(8,128)}, u32[]{:S(2)}, u32[]{:S(2)}) collective-permute-start(f32[6,128,128]{2,1,0:T(8,128)} %get-tuple-element.74), channel_id=1, source_target_pairs={{8,0},{9,1},{10,2},{11,3},{12,4},{13,5},{14,6},{15,7},{16,8},{17,9... | collective-permute-start | bytes 1179656 | tf_op jit(solution)/shard_map/ppermute | solution.py:16
  618.8 15.9 %copy-start.5 = (f32[6,128,128]{2,1,0:T(8,128)}, f32[6,128,128]{2,1,0:T(8,128)S(1)}, u32[]{:S(2)}) copy-start(f32[6,128,128]{2,1,0:T(8,128)S(1)} %collective-permute-done.6) | copy-start | bytes 1179652
  636.1 0.7 copy-start
  636.9 173.9 %all-gather.15.cloned.1.call-start = ((), (), s32[]{:S(2)}) async-start(), calls=%async_computation.7 | async-start | bytes 2359296 | tf_op jit(solution)/shard_map/all_gather | solution.py:8
  815.8 12.3 %collective-permute-start.10 = (f32[6,128,128]{2,1,0:T(8,128)}, f32[6,128,128]{2,1,0:T(8,128)}, u32[]{:S(2)}, u32[]{:S(2)}) collective-permute-start(f32[6,128,128]{2,1,0:T(8,128)} %get-tuple-element.72), channel_id=1, source_target_pairs={{16,0},{17,1},{18,2},{19,3},{20,4},{21,5},{22,6},{23,7},{24,8},{25... | collective-permute-start | bytes 1179656 | tf_op jit(solution)/shard_map/ppermute | solution.py:16
  818.5 25.1 %collective-permute-start.11 = (f32[6,128,128]{2,1,0:T(8,128)}, f32[6,128,128]{2,1,0:T(8,128)}, u32[]{:S(2)}, u32[]{:S(2)}) collective-permute-start(f32[6,128,128]{2,1,0:T(8,128)} %get-tuple-element.71), channel_id=1, source_target_pairs={{8,0},{9,1},{10,2},{11,3},{12,4},{13,5},{14,6},{15,7},{16,8},{17,9... | collective-permute-start | bytes 1179656 | tf_op jit(solution)/shard_map/ppermute | solution.py:16
  825.2 18.3 %collective-permute-start.9 = (f32[6,128,128]{2,1,0:T(8,128)}, f32[6,128,128]{2,1,0:T(8,128)}, u32[]{:S(2)}, u32[]{:S(2)}) collective-permute-start(f32[6,128,128]{2,1,0:T(8,128)} %get-tuple-element.70), channel_id=1, source_target_pairs={{24,0},{25,1},{26,2},{27,3},{28,4},{29,5},{30,6},{31,7},{0,8},{1,9... | collective-permute-start | bytes 1179656 | tf_op jit(solution)/shard_map/ppermute | solution.py:16
Sparse Core Ops, SparseCore 0:
  12.0 142.6 all-reduce.4
  158.1 28.5 all-gather.8
  221.5 140.8 all-reduce.6
  365.8 28.5 all-gather.10
  427.8 141.9 all-reduce.8
  573.2 28.5 all-gather.12
  637.0 141.7 all-reduce.10
  782.1 28.5 all-gather.14
